TPU v7x, 256 devices: a whole 4x4x8 slice. The times are simulated.
256 devices in a mesh: rows: 32 (over x, z), vecs: 8 (over y, core).
Axes of the slice: x: 4, y: 4, z: 8, core: 2. Of those that a mesh axis runs over, the one named last changes fastest.
Arguments:
- coords: float32 [3, 8192], P(None, ('rows', 'vecs')), may hold values from 0 to 1
- old_vectors: bfloat16 [8192, 16384], P('rows', 'vecs'), may hold values from -0.078125 to 0.078125
- pivots: int32 [2, 128], replicated, may hold values from 0 to 8191, as said below
- slots: int32 [8192], replicated, may hold values from 0 to 8191, each once
Outputs:
- new_vectors: float32 [8192, 256], P(('rows', 'vecs'))
Inputs may be any that keep to these rules, and one draw needn't show every extreme that they name: `pivots`: all 256 pivot numbers are distinct. `slots`: each window row belongs to exactly one point.
All inputs are finite; a program needn't handle non-finite values.
Results may differ from a plain program's by a relative error of at most 0.0003.
Values may be sent and summed in bfloat16 or wider, within the bound.
A program may use at most 64 MiB of HBM per device.

v0:
```python
import jax
import jax.numpy as jnp
from jax import lax
from jax.sharding import PartitionSpec as P

length_scale = 0.5
noise_shift = 12.0


def matern(points, centers):
    dist_sq = jnp.zeros((points.shape[1], centers.shape[1]), jnp.float32)
    for component in range(3):
        differ = points[component][:, None] - centers[component][None, :]
        dist_sq = dist_sq + differ * differ
    scaled = jnp.sqrt(5.0 * dist_sq) / length_scale
    return (1.0 + scaled + scaled * scaled / 3.0) * jnp.exp(-scaled)


def pick_rows(block_data, wanted, first_row):
    length = block_data.shape[0]
    offset = wanted - first_row
    inside = (offset >= 0) & (offset < length)
    bounded = jnp.clip(offset, 0, length - 1)
    fetched = jnp.take(block_data, bounded, axis=0)
    return jnp.where(inside[:, None], fetched, jnp.zeros((), block_data.dtype))


def shards(coords, old_vectors, pivots, slots):
    row_block = old_vectors.shape[0]
    share = coords.shape[1]
    panels = pivots.shape[0]
    width = pivots.shape[1]
    block_first = lax.axis_index("rows") * row_block
    share_first = block_first + lax.axis_index("vecs") * share
    wanted = jnp.take(slots, pivots.reshape(-1), axis=0)
    my_rows = share_first + jnp.arange(share, dtype=jnp.int32)
    every_point = lax.all_gather(coords, ("rows", "vecs"), axis=1, tiled=True)
    centers = jnp.take(every_point, wanted, axis=1)
    new_panels = []
    for panel in range(panels):
        chosen = wanted[panel * width : (panel + 1) * width]
        old_pivot = (
            lax.psum(pick_rows(old_vectors, chosen, block_first), "rows")
            .astype(jnp.float32)
            .astype(jnp.bfloat16)
        )

        def residual_term(first_row, length, old_pivot=old_pivot):
            return jnp.dot(old_vectors, old_pivot.T, preferred_element_type=jnp.float32)

        summed = lax.psum_scatter(
            residual_term(jnp.int32(0), share * lax.axis_size("vecs")),
            "vecs",
            scatter_dimension=0,
            tiled=True,
        )
        kernel = matern(coords, centers[:, panel * width : (panel + 1) * width])
        kernel = kernel + noise_shift * (my_rows[:, None] == chosen[None, :]).astype(jnp.float32)
        current = kernel - summed
        if panel > 0:
            stacked = new_panels[0]
            earlier = lax.psum(pick_rows(stacked, chosen, share_first), ("rows", "vecs"))
            current = current - jnp.dot(
                stacked,
                earlier.T,
                precision=lax.Precision.HIGHEST,
                preferred_element_type=jnp.float32,
            )
        block = lax.psum(pick_rows(current, chosen, share_first), ("rows", "vecs"))
        factor = jnp.linalg.cholesky(block)
        fresh = jax.scipy.linalg.solve_triangular(factor, current.T, lower=True).T
        new_panels.append(fresh)
    return jnp.concatenate(new_panels, axis=1)


def solution(mesh):
    in_specs = (P(None, ("rows", "vecs")), P("rows", "vecs"), P(), P())
    out_specs = P(("rows", "vecs"), None)
    return jax.shard_map(shards, mesh=mesh, in_specs=in_specs, out_specs=out_specs, check_vma=False)
```

profile of v0, /device:TPU:1, one launch (start us, length us, event | category | flops | bytes accessed | tf_op | source)
XLA Modules:
  0.0 1000.4 jit_solution(14306244718149790146)
XLA Ops:
  6.5 0.8 compare_select_fusion.1
  7.3 2.0 gather_fusion
  9.3 0.7 compare_and_fusion.7
  10.1 0.9 gather_fusion.4
  11.0 0.9 gather_fusion.2
  12.0 1.2 select_select_fusion
  13.2 73.2 %all-gather = f32[256,32,3]{1,2,0:T(4,128)S(1)} all-gather(f32[1,32,3]{1,2,0:T(4,128)S(1)} %bitcast.66), channel_id=1, replica_groups=mesh['rows'=32,'vecs'=8] {'rows','vecs'}, dimensions={0}, use_global_device_ids=true | all-gather | bytes 98688 | tf_op jit(solution)/shard_map/all_gather | solution.py:37
  86.5 3.0 copy.23
  89.5 2.9 gather_fusion.1
  92.4 0.1 select_bitcast_fusion
  92.5 0.3 slice_reduce_fusion.2
  92.8 70.1 %all-reduce.12.cloned.1.call-done = (bf16[128,2048]{1,0:T(8,128)(2,1)}, bf16[128,2048]{1,0:T(8,128)(2,1)}) async-done(((bf16[128,2048]{1,0:T(8,128)(2,1)}, bf16[128,2048]{1,0:T(8,128)(2,1)}), (bf16[128,2048]{1,0:T(8,128)(2,1)}, bf16[128,2048]{1,0:T(8,128)(2,1)})) %all-reduce.12.cloned.1.call-update) | async-done | bytes 1048592 | tf_op jit(solution)/shard_map/psum | solution.py:43
  162.9 1.5 convolution_bitcast_fusion.1
  164.4 0.7 copy.31
  165.3 33.3 %reduce-scatter.7.cloned.1.call-done = f32[32,128]{1,0:T(8,128)} async-done(((f32[256,128]{1,0:T(8,128)}), f32[32,128]{1,0:T(8,128)}) %reduce-scatter.7.cloned.1.call-update) | async-done | bytes 16400 | tf_op jit(solution)/shard_map/reduce_scatter | solution.py:51
  198.5 0.8 add_subtract_fusion
  199.3 0.6 gather_fusion.3
  200.0 0.1 copy.25
  200.1 0.6 select_select_fusion.6
  200.8 1.5 convolution_bitcast_fusion
  202.3 0.7 copy.33
  203.1 243.7 %all-reduce.6.cloned.1.call-done = f32[128,128]{0,1:T(8,128)} async-done(((f32[128,128]{0,1:T(8,128)}), f32[128,128]{0,1:T(8,128)}) %all-reduce.6.cloned.1.call-update) | async-done | bytes 65552 | tf_op jit(solution)/shard_map/psum | solution.py:69
  446.9 0.9 copy.26
  447.8 0.9 fusion.6
  448.6 11.7 %cholesky.44 = f32[128,128]{1,0:T(8,128)S(1)} custom-call(f32[128,128]{1,0:T(8,128)S(1)} %fusion.6), custom_call_target="Cholesky" | custom-call | tf_op jit(solution)/shard_map/jit(cholesky)/cholesky | solution.py:70
  460.4 0.6 compare_reduce_fusion.1
  461.0 0.7 fusion
  461.7 9.8 custom-call.6
  471.5 0.2 fusion.4
  471.7 0.7 gather_fusion.5
  472.3 0.1 copy.28
  472.4 0.6 select_select_fusion.5
  473.1 0.2 all-reduce.10.cloned.1.call-start
  473.3 3.4 reduce-scatter.9.cloned.1.call-done
  476.7 248.0 %all-reduce.8.cloned.1.call-done = f32[128,128]{0,1:T(8,128)} async-done(((f32[128,128]{0,1:T(8,128)}), f32[128,128]{0,1:T(8,128)}) %all-reduce.8.cloned.1.call-update) | async-done | bytes 65552 | tf_op jit(solution)/shard_map/psum | solution.py:62
  724.8 1.0 convolution_subtract_fusion
  725.8 0.6 gather_fusion.6
  726.5 0.1 copy.29
  726.6 0.6 select_select_fusion.4
  727.2 240.9 %all-reduce.10.cloned.1.call-done = f32[128,128]{0,1:T(8,128)} async-done(((f32[128,128]{0,1:T(8,128)}), f32[128,128]{0,1:T(8,128)}) %all-reduce.10.cloned.1.call-update) | async-done | bytes 65552 | tf_op jit(solution)/shard_map/psum | solution.py:69
  968.1 0.9 copy.30
  969.0 0.9 fusion.3
  969.9 11.7 %cholesky.55 = f32[128,128]{1,0:T(8,128)S(1)} custom-call(f32[128,128]{1,0:T(8,128)S(1)} %fusion.3), custom_call_target="Cholesky" | custom-call | tf_op jit(solution)/shard_map/jit(cholesky)/cholesky | solution.py:70
  981.6 0.6 compare_reduce_fusion
  982.3 0.7 fusion.1
  983.0 9.8 custom-call.7
  992.8 0.2 convolution_bitcast_fusion.2
  992.9 0.6 pad_maximum_fusion
  (30 shorter events, 0.4 us)
Async XLA Ops:
  6.5 3.5 copy-start
  6.5 156.3 %all-reduce.12.cloned.1.call-start = ((), (), s32[]{:S(2)}) async-start(), calls=%async_computation.7 | async-start | bytes 2097152 | tf_op jit(solution)/shard_map/psum | solution.py:43
  11.0 2.2 copy-start.2
  12.0 77.5 %copy-start.1 = (s32[2,128]{1,0:T(2,128)S(1)}, s32[2,128]{1,0:T(2,128)}, u32[]{:S(2)}) copy-start(s32[2,128]{1,0:T(2,128)} %param.13) | copy-start | bytes 3076
  13.2 185.3 %reduce-scatter.7.cloned.1.call-start = ((), (), s32[]{:S(2)}) async-start(), calls=%async_computation.5 | async-start | bytes 147456 | tf_op jit(solution)/shard_map/reduce_scatter | solution.py:51
  165.2 281.7 %all-reduce.6.cloned.1.call-start = ((), (), s32[]{:S(2)}) async-start(), calls=%async_computation.2 | async-start | bytes 131072 | tf_op jit(solution)/shard_map/psum | solution.py:69
  200.7 276.0 %reduce-scatter.9.cloned.1.call-start = ((), (), s32[]{:S(2)}) async-start(), calls=%async_computation.6 | async-start | bytes 147456 | tf_op jit(solution)/shard_map/reduce_scatter | solution.py:51
  203.1 521.7 %all-reduce.8.cloned.1.call-start = ((), (), s32[]{:S(2)}) async-start(), calls=%async_computation.3 | async-start | bytes 131072 | tf_op jit(solution)/shard_map/psum | solution.py:62
  473.1 495.0 %all-reduce.10.cloned.1.call-start = ((), (), s32[]{:S(2)}) async-start(), calls=%async_computation.4 | async-start | bytes 131072 | tf_op jit(solution)/shard_map/psum | solution.py:69
Sparse Core Ops, SparseCore 0:
  13.3 149.5 all-reduce.11
  165.4 33.0 reduce-scatter.6
  204.0 242.7 all-reduce.5
  449.2 27.4 reduce-scatter.8
  482.1 242.6 all-reduce.7
  730.2 237.9 all-reduce.9
where the time goes:
time: 1000 us
  waiting for transfers between devices  840 us (84%)
  blocking collectives  73.2 us (7%)
  other arithmetic  53.6 us (5%)
  local copies, waits for them, and re-layouts  15.6 us (2%)
  between operations  13.7 us (1%)
    psum x2, waiting for transfers between devices, shards(): block = lax.psum(pick_rows(current, chosen, share_first), ('rows', 'vecs'))  485 us
    psum x1, waiting for transfers between devices, shards(): lax.psum(pick_rows(stacked, chosen, share_first), ('rows', 'vecs'))  248 us
    all_gather x1, blocking collectives, shards(): every_point = lax.all_gather(coords, ('rows', 'vecs'), axis=1, tiled=True)  73.2 us
    psum x1, waiting for transfers between devices, shards(): lax.psum(pick_rows(old_vectors, chosen, block_first), 'rows')  70.1 us
    reduce_scatter x2, waiting for transfers between devices, shards(): lax.psum_scatter(residual_term(jnp.int32(0), share * lax.axis_size('vecs'...  36.7 us
    another operation x6, other arithmetic, shards(): factor = jnp.linalg.cholesky(block)  24.8 us
    another operation x4, other arithmetic, shards(): fresh = jax.scipy.linalg.solve_triangular(factor, current.T, lower=True).T  20.9 us
  transfers between devices with their start and end apart: 6, of which 6 were waited for; matrix products, arithmetic and copies ran while one was open for 3% of the time, Pallas kernels for 0%

commit v1 on v0

--- a/solution.py
+++ b/solution.py
@@ -66,7 +66,8 @@
                 precision=lax.Precision.HIGHEST,
                 preferred_element_type=jnp.float32,
             )
-        block = lax.psum(pick_rows(current, chosen, share_first), ("rows", "vecs"))
+        partial = lax.psum(pick_rows(current, chosen, share_first), "rows")
+        block = lax.psum(partial, "vecs")
         factor = jnp.linalg.cholesky(block)
         fresh = jax.scipy.linalg.solve_triangular(factor, current.T, lower=True).T
         new_panels.append(fresh)

time: 1000 us -> 929 us (0.929)
  waiting for transfers between devices: 840 us -> 766 us
    psum x2 -> x4, waiting for transfers between devices: 485 us -> 406 us  [the longest x2 273 us: shards(): partial = lax.psum(pick_rows(current, chosen, share_first), 'rows')]
  transfers between devices with their start and end apart: 6 -> 8, of which waited for: 6 -> 8; matrix products, arithmetic and copies ran while one was open for 3% -> 4% of each run, Pallas kernels for 0% -> 0%
where the time goes in v1:
time: 929 us; the launch traced here: 927 us
  waiting for transfers between devices  766 us (82%)
  blocking collectives  73.2 us (8%)
  other arithmetic  53.6 us (6%)
  local copies, waits for them, and re-layouts  15.6 us (2%)
  between operations  13.7 us (1%)
    psum x2, waiting for transfers between devices, shards(): partial = lax.psum(pick_rows(current, chosen, share_first), 'rows')  273 us
    psum x1, waiting for transfers between devices, shards(): lax.psum(pick_rows(stacked, chosen, share_first), ('rows', 'vecs'))  248 us
    psum x2, waiting for transfers between devices, shards(): block = lax.psum(partial, 'vecs')  133 us
    all_gather x1, blocking collectives, shards(): every_point = lax.all_gather(coords, ('rows', 'vecs'), axis=1, tiled=True)  73.2 us
    psum x1, waiting for transfers between devices, shards(): lax.psum(pick_rows(old_vectors, chosen, block_first), 'rows')  70.1 us
    reduce_scatter x2, waiting for transfers between devices, shards(): lax.psum_scatter(residual_term(jnp.int32(0), share * lax.axis_size('vecs'...  41.7 us
    another operation x6, other arithmetic, shards(): factor = jnp.linalg.cholesky(block)  24.8 us
    another operation x4, other arithmetic, shards(): fresh = jax.scipy.linalg.solve_triangular(factor, current.T, lower=True).T  20.9 us
  transfers between devices with their start and end apart: 8, of which 8 were waited for; matrix products, arithmetic and copies ran while one was open for 4% of the time, Pallas kernels for 0%

profile of v1, /device:TPU:1, one launch (start us, length us, event | category | flops | bytes accessed | tf_op | source)
XLA Modules:
  0.0 927.4 jit_solution(8206328812932801323)
XLA Ops:
  6.5 0.8 compare_select_fusion.1
  7.3 2.0 gather_fusion
  9.3 0.7 compare_and_fusion.7
  10.1 0.9 gather_fusion.4
  11.0 0.9 gather_fusion.2
  12.0 1.2 select_select_fusion
  13.2 73.2 %all-gather = f32[256,32,3]{1,2,0:T(4,128)S(1)} all-gather(f32[1,32,3]{1,2,0:T(4,128)S(1)} %bitcast.66), channel_id=1, replica_groups=mesh['rows'=32,'vecs'=8] {'rows','vecs'}, dimensions={0}, use_global_device_ids=true | all-gather | bytes 98688 | tf_op jit(solution)/shard_map/all_gather | solution.py:37
  86.5 3.0 copy.23
  89.5 2.9 gather_fusion.1
  92.4 0.1 select_bitcast_fusion
  92.5 0.3 slice_reduce_fusion.2
  92.8 70.1 %all-reduce.18.cloned.1.call-done = (bf16[128,2048]{1,0:T(8,128)(2,1)}, bf16[128,2048]{1,0:T(8,128)(2,1)}) async-done(((bf16[128,2048]{1,0:T(8,128)(2,1)}, bf16[128,2048]{1,0:T(8,128)(2,1)}), (bf16[128,2048]{1,0:T(8,128)(2,1)}, bf16[128,2048]{1,0:T(8,128)(2,1)})) %all-reduce.18.cloned.1.call-update) | async-done | bytes 1048592 | tf_op jit(solution)/shard_map/psum | solution.py:43
  162.9 1.5 convolution_bitcast_fusion.1
  164.4 0.7 copy.31
  165.3 33.3 %reduce-scatter.7.cloned.1.call-done = f32[32,128]{1,0:T(8,128)} async-done(((f32[256,128]{1,0:T(8,128)}), f32[32,128]{1,0:T(8,128)}) %reduce-scatter.7.cloned.1.call-update) | async-done | bytes 16400 | tf_op jit(solution)/shard_map/reduce_scatter | solution.py:51
  198.5 0.8 add_subtract_fusion
  199.3 0.6 gather_fusion.3
  200.0 0.1 copy.25
  200.1 0.6 select_select_fusion.6
  200.8 139.3 %all-reduce.8.cloned.1.call-done = f32[128,128]{0,1:T(8,128)} async-done(((f32[128,128]{0,1:T(8,128)}), f32[128,128]{0,1:T(8,128)}) %all-reduce.8.cloned.1.call-update) | async-done | bytes 65552 | tf_op jit(solution)/shard_map/psum | solution.py:69
  340.2 1.5 convolution_bitcast_fusion
  341.7 0.7 copy.33
  342.5 65.2 %all-reduce.10.cloned.1.call-done = f32[128,128]{0,1:T(8,128)} async-done(((f32[128,128]{0,1:T(8,128)}), f32[128,128]{0,1:T(8,128)}) %all-reduce.10.cloned.1.call-update) | async-done | bytes 65552 | tf_op jit(solution)/shard_map/psum | solution.py:70
  407.7 0.9 copy.26
  408.7 0.9 fusion.6
  409.5 11.7 %cholesky.44 = f32[128,128]{1,0:T(8,128)S(1)} custom-call(f32[128,128]{1,0:T(8,128)S(1)} %fusion.6), custom_call_target="Cholesky" | custom-call | tf_op jit(solution)/shard_map/jit(cholesky)/cholesky | solution.py:71
  421.3 0.6 compare_reduce_fusion.1
  421.9 0.7 fusion
  422.6 9.8 %custom-call.6 = f32[1,128,128]{1,2,0:T(8,128)S(1)} custom-call(f32[1,128,128]{2,1,0:T(8,128)S(1)} %fusion), custom_call_target="InvertDiagBlocksLowerTriangular" | custom-call | tf_op jit(solution)/shard_map/jit(_solve_triangular)/triangular_solve | solution.py:72
  432.4 0.2 fusion.4
  432.6 0.7 gather_fusion.5
  433.3 0.6 select_select_fusion.5
  434.0 8.4 reduce-scatter.9.cloned.1.call-done
  442.4 248.2 %all-reduce.12.cloned.1.call-done = f32[128,128]{0,1:T(8,128)} async-done(((f32[128,128]{0,1:T(8,128)}), f32[128,128]{0,1:T(8,128)}) %all-reduce.12.cloned.1.call-update) | async-done | bytes 65552 | tf_op jit(solution)/shard_map/psum | solution.py:62
  690.7 1.0 convolution_subtract_fusion
  691.7 0.6 gather_fusion.6
  692.4 0.6 select_select_fusion.4
  693.1 0.2 all-reduce.16.cloned.1.call-start
  693.3 134.0 %all-reduce.14.cloned.1.call-done = f32[128,128]{0,1:T(8,128)} async-done(((f32[128,128]{0,1:T(8,128)}), f32[128,128]{0,1:T(8,128)}) %all-reduce.14.cloned.1.call-update) | async-done | bytes 65552 | tf_op jit(solution)/shard_map/psum | solution.py:69
  827.4 67.7 %all-reduce.16.cloned.1.call-done = f32[128,128]{0,1:T(8,128)} async-done(((f32[128,128]{0,1:T(8,128)}), f32[128,128]{0,1:T(8,128)}) %all-reduce.16.cloned.1.call-update) | async-done | bytes 65552 | tf_op jit(solution)/shard_map/psum | solution.py:70
  895.1 0.9 copy.30
  896.0 0.9 fusion.3
  896.9 11.7 %cholesky.55 = f32[128,128]{1,0:T(8,128)S(1)} custom-call(f32[128,128]{1,0:T(8,128)S(1)} %fusion.3), custom_call_target="Cholesky" | custom-call | tf_op jit(solution)/shard_map/jit(cholesky)/cholesky | solution.py:71
  908.6 0.6 compare_reduce_fusion
  909.3 0.7 fusion.1
  909.9 9.8 %custom-call.7 = f32[1,128,128]{1,2,0:T(8,128)S(1)} custom-call(f32[1,128,128]{2,1,0:T(8,128)S(1)} %fusion.1), custom_call_target="InvertDiagBlocksLowerTriangular" | custom-call | tf_op jit(solution)/shard_map/jit(_solve_triangular)/triangular_solve | solution.py:72
  919.8 0.2 convolution_bitcast_fusion.2
  919.9 0.6 pad_maximum_fusion
  (36 shorter events, 0.7 us)
Async XLA Ops:
  6.5 3.5 copy-start
  6.5 156.3 %all-reduce.18.cloned.1.call-start = ((), (), s32[]{:S(2)}) async-start(), calls=%async_computation.9 | async-start | bytes 2097152 | tf_op jit(solution)/shard_map/psum | solution.py:43
  11.0 2.2 copy-start.2
  12.0 77.5 %copy-start.1 = (s32[2,128]{1,0:T(2,128)S(1)}, s32[2,128]{1,0:T(2,128)}, u32[]{:S(2)}) copy-start(s32[2,128]{1,0:T(2,128)} %param.13) | copy-start | bytes 3076
  13.2 185.3 %reduce-scatter.7.cloned.1.call-start = ((), (), s32[]{:S(2)}) async-start(), calls=%async_computation.7 | async-start | bytes 147456 | tf_op jit(solution)/shard_map/reduce_scatter | solution.py:51
  165.2 174.9 %all-reduce.8.cloned.1.call-start = ((), (), s32[]{:S(2)}) async-start(), calls=%async_computation.2 | async-start | bytes 131072 | tf_op jit(solution)/shard_map/psum | solution.py:69
  200.7 207.0 %all-reduce.10.cloned.1.call-start = ((), (), s32[]{:S(2)}) async-start(), calls=%async_computation.3 | async-start | bytes 131072 | tf_op jit(solution)/shard_map/psum | solution.py:70
  340.1 102.3 %reduce-scatter.9.cloned.1.call-start = ((), (), s32[]{:S(2)}) async-start(), calls=%async_computation.8 | async-start | bytes 147456 | tf_op jit(solution)/shard_map/reduce_scatter | solution.py:51
  342.5 348.2 %all-reduce.12.cloned.1.call-start = ((), (), s32[]{:S(2)}) async-start(), calls=%async_computation.4 | async-start | bytes 131072 | tf_op jit(solution)/shard_map/psum | solution.py:62
  434.0 393.4 %all-reduce.14.cloned.1.call-start = ((), (), s32[]{:S(2)}) async-start(), calls=%async_computation.5 | async-start | bytes 131072 | tf_op jit(solution)/shard_map/psum | solution.py:69
  693.1 202.0 %all-reduce.16.cloned.1.call-start = ((), (), s32[]{:S(2)}) async-start(), calls=%async_computation.6 | async-start | bytes 131072 | tf_op jit(solution)/shard_map/psum | solution.py:70
Sparse Core Ops, SparseCore 0:
  13.3 149.5 all-reduce.17
  165.4 33.0 reduce-scatter.6
  202.0 138.1 all-reduce.7
  342.3 65.3 all-reduce.9
  410.1 32.3 reduce-scatter.8
  447.8 242.8 all-reduce.11
  694.1 133.1 all-reduce.13
  829.7 65.3 all-reduce.15

commit v2 on v0

--- a/solution.py
+++ b/solution.py
@@ -5,6 +5,11 @@
 
 length_scale = 0.5
 noise_shift = 12.0
+
+
+def axis_by_axis(array, first, second):
+    half = lax.psum(array, first)
+    return lax.psum(half, second)
 
 
 def matern(points, centers):
@@ -59,7 +64,7 @@
         current = kernel - summed
         if panel > 0:
             stacked = new_panels[0]
-            earlier = lax.psum(pick_rows(stacked, chosen, share_first), ("rows", "vecs"))
+            earlier = axis_by_axis(pick_rows(stacked, chosen, share_first), "rows", "vecs")
             current = current - jnp.dot(
                 stacked,
                 earlier.T,

time: 1000 us -> 990 us (0.990)
  waiting for transfers between devices: 840 us -> 829 us
    psum x1 -> x2, waiting for transfers between devices: 248 us -> 198 us  [the longest x1 132 us: axis_by_axis(): half = lax.psum(array, first)]
    reduce_scatter x2, waiting for transfers between devices: 36.7 us -> 68.9 us  [shards(): lax.psum_scatter(residual_term(jnp.int32(0), share * lax.axis_size('vecs'...]
  transfers between devices with their start and end apart: 6 -> 7, of which waited for: 6 -> 7; matrix products, arithmetic and copies ran while one was open for 3% -> 1% of each run, Pallas kernels for 0% -> 0%
where the time goes in v2:
time: 990 us; the launch traced here: 989 us
  waiting for transfers between devices  829 us (84%)
  blocking collectives  73.2 us (7%)
  other arithmetic  53.6 us (5%)
  local copies, waits for them, and re-layouts  15.6 us (2%)
  between operations  13.7 us (1%)
    psum x2, waiting for transfers between devices, shards(): block = lax.psum(pick_rows(current, chosen, share_first), ('rows', 'vecs'))  492 us
    psum x1, waiting for transfers between devices, axis_by_axis(): half = lax.psum(array, first)  132 us
    all_gather x1, blocking collectives, shards(): every_point = lax.all_gather(coords, ('rows', 'vecs'), axis=1, tiled=True)  73.2 us
    psum x1, waiting for transfers between devices, shards(): lax.psum(pick_rows(old_vectors, chosen, block_first), 'rows')  70.1 us
    reduce_scatter x2, waiting for transfers between devices, shards(): lax.psum_scatter(residual_term(jnp.int32(0), share * lax.axis_size('vecs'...  68.9 us
    psum x1, waiting for transfers between devices, axis_by_axis(): return lax.psum(half, second)  66.1 us
    another operation x6, other arithmetic, shards(): factor = jnp.linalg.cholesky(block)  24.8 us
    another operation x4, other arithmetic, shards(): fresh = jax.scipy.linalg.solve_triangular(factor, current.T, lower=True).T  20.9 us
  transfers between devices with their start and end apart: 7, of which 7 were waited for; matrix products, arithmetic and copies ran while one was open for 1% of the time, Pallas kernels for 0%

profile of v2, /device:TPU:1, one launch (start us, length us, event | category | flops | bytes accessed | tf_op | source)
XLA Modules:
  0.0 989.3 jit_solution(2948837148954142427)
XLA Ops:
  6.5 0.8 compare_select_fusion.1
  7.3 2.0 gather_fusion
  9.3 0.7 compare_and_fusion.7
  10.1 0.9 gather_fusion.4
  11.0 0.9 gather_fusion.2
  12.0 1.2 select_select_fusion
  13.2 73.2 %all-gather = f32[256,32,3]{1,2,0:T(4,128)S(1)} all-gather(f32[1,32,3]{1,2,0:T(4,128)S(1)} %bitcast.66), channel_id=1, replica_groups=mesh['rows'=32,'vecs'=8] {'rows','vecs'}, dimensions={0}, use_global_device_ids=true | all-gather | bytes 98688 | tf_op jit(solution)/shard_map/all_gather | solution.py:42
  86.5 3.0 copy.23
  89.5 2.9 gather_fusion.1
  92.4 0.1 select_bitcast_fusion
  92.5 0.3 slice_reduce_fusion.2
  92.8 70.1 %all-reduce.15.cloned.1.call-done = (bf16[128,2048]{1,0:T(8,128)(2,1)}, bf16[128,2048]{1,0:T(8,128)(2,1)}) async-done(((bf16[128,2048]{1,0:T(8,128)(2,1)}, bf16[128,2048]{1,0:T(8,128)(2,1)}), (bf16[128,2048]{1,0:T(8,128)(2,1)}, bf16[128,2048]{1,0:T(8,128)(2,1)})) %all-reduce.15.cloned.1.call-update) | async-done | bytes 1048592 | tf_op jit(solution)/shard_map/psum | solution.py:48
  162.9 1.6 convolution_bitcast_fusion.1
  164.5 0.7 copy.31
  165.3 33.2 %reduce-scatter.7.cloned.1.call-done = f32[32,128]{1,0:T(8,128)} async-done(((f32[256,128]{1,0:T(8,128)}), f32[32,128]{1,0:T(8,128)}) %reduce-scatter.7.cloned.1.call-update) | async-done | bytes 16400 | tf_op jit(solution)/shard_map/reduce_scatter | solution.py:56
  198.5 0.8 add_subtract_fusion
  199.3 0.6 gather_fusion.3
  200.0 0.1 copy.25
  200.1 0.6 select_select_fusion.6
  200.8 246.1 %all-reduce.7.cloned.1.call-done = f32[128,128]{0,1:T(8,128)} async-done(((f32[128,128]{0,1:T(8,128)}), f32[128,128]{0,1:T(8,128)}) %all-reduce.7.cloned.1.call-update) | async-done | bytes 65552 | tf_op jit(solution)/shard_map/psum | solution.py:74
  446.9 0.9 copy.26
  447.8 0.9 fusion.6
  448.7 11.7 %cholesky.44 = f32[128,128]{1,0:T(8,128)S(1)} custom-call(f32[128,128]{1,0:T(8,128)S(1)} %fusion.6), custom_call_target="Cholesky" | custom-call | tf_op jit(solution)/shard_map/jit(cholesky)/cholesky | solution.py:75
  460.4 0.6 compare_reduce_fusion.1
  461.1 0.7 fusion
  461.7 9.8 custom-call.6
  471.6 0.2 fusion.4
  471.7 0.7 gather_fusion.5
  472.4 0.1 copy.28
  472.5 0.6 select_select_fusion.5
  473.2 0.5 convolution_bitcast_fusion
  473.7 0.7 copy.33
  474.5 132.0 %all-reduce.9.cloned.1.call-done = f32[128,128]{0,1:T(8,128)} async-done(((f32[128,128]{0,1:T(8,128)}), f32[128,128]{0,1:T(8,128)}) %all-reduce.9.cloned.1.call-update) | async-done | bytes 65552 | tf_op jit(solution)/shard_map/psum | solution.py:11
  606.5 0.2 all-reduce.13.cloned.1.call-start
  606.7 35.7 %reduce-scatter.9.cloned.1.call-done = f32[32,128]{1,0:T(8,128)} async-done(((f32[256,128]{1,0:T(8,128)}), f32[32,128]{1,0:T(8,128)}) %reduce-scatter.9.cloned.1.call-update) | async-done | bytes 16400 | tf_op jit(solution)/shard_map/reduce_scatter | solution.py:56
  642.5 66.1 %all-reduce.11.cloned.1.call-done = f32[128,128]{0,1:T(8,128)} async-done(((f32[128,128]{0,1:T(8,128)}), f32[128,128]{0,1:T(8,128)}) %all-reduce.11.cloned.1.call-update) | async-done | bytes 65552 | tf_op jit(solution)/shard_map/psum | solution.py:12
  708.6 1.0 convolution_subtract_fusion
  709.6 0.6 gather_fusion.6
  710.4 0.6 select_select_fusion.4
  711.0 245.9 %all-reduce.13.cloned.1.call-done = f32[128,128]{0,1:T(8,128)} async-done(((f32[128,128]{0,1:T(8,128)}), f32[128,128]{0,1:T(8,128)}) %all-reduce.13.cloned.1.call-update) | async-done | bytes 65552 | tf_op jit(solution)/shard_map/psum | solution.py:74
  957.0 0.9 copy.30
  957.9 0.9 fusion.3
  958.8 11.7 %cholesky.55 = f32[128,128]{1,0:T(8,128)S(1)} custom-call(f32[128,128]{1,0:T(8,128)S(1)} %fusion.3), custom_call_target="Cholesky" | custom-call | tf_op jit(solution)/shard_map/jit(cholesky)/cholesky | solution.py:75
  970.5 0.6 compare_reduce_fusion
  971.1 0.7 fusion.1
  971.8 9.8 custom-call.7
  981.6 0.2 convolution_bitcast_fusion.2
  981.8 0.6 pad_maximum_fusion
  (35 shorter events, 0.6 us)
Async XLA Ops:
  6.5 3.5 copy-start
  6.5 156.3 %all-reduce.15.cloned.1.call-start = ((), (), s32[]{:S(2)}) async-start(), calls=%async_computation.8 | async-start | bytes 2097152 | tf_op jit(solution)/shard_map/psum | solution.py:48
  11.0 2.2 copy-start.3
  12.0 77.5 %copy-start.2 = (s32[2,128]{1,0:T(2,128)S(1)}, s32[2,128]{1,0:T(2,128)}, u32[]{:S(2)}) copy-start(s32[2,128]{1,0:T(2,128)} %param.13) | copy-start | bytes 3076
  13.2 185.3 %reduce-scatter.7.cloned.1.call-start = ((), (), s32[]{:S(2)}) async-start(), calls=%async_computation.6 | async-start | bytes 147456 | tf_op jit(solution)/shard_map/reduce_scatter | solution.py:56
  162.9 310.3 %copy-start.1 = (bf16[128,2048]{1,0:T(8,128)(2,1)S(1)}, bf16[128,2048]{1,0:T(8,128)(2,1)}, u32[]{:S(2)}) copy-start(bf16[128,2048]{1,0:T(8,128)(2,1)} %get-tuple-element.16) | copy-start | bytes 1572868
  165.2 281.7 %all-reduce.7.cloned.1.call-start = ((), (), s32[]{:S(2)}) async-start(), calls=%async_computation.2 | async-start | bytes 131072 | tf_op jit(solution)/shard_map/psum | solution.py:74
  200.7 405.8 %all-reduce.9.cloned.1.call-start = ((), (), s32[]{:S(2)}) async-start(), calls=%async_computation.3 | async-start | bytes 131072 | tf_op jit(solution)/shard_map/psum | solution.py:11
  473.1 169.4 %reduce-scatter.9.cloned.1.call-start = ((), (), s32[]{:S(2)}) async-start(), calls=%async_computation.7 | async-start | bytes 147456 | tf_op jit(solution)/shard_map/reduce_scatter | solution.py:56
  474.4 234.2 %all-reduce.11.cloned.1.call-start = ((), (), s32[]{:S(2)}) async-start(), calls=%async_computation.4 | async-start | bytes 131072 | tf_op jit(solution)/shard_map/psum | solution.py:12
  606.5 350.4 %all-reduce.13.cloned.1.call-start = ((), (), s32[]{:S(2)}) async-start(), calls=%async_computation.5 | async-start | bytes 131072 | tf_op jit(solution)/shard_map/psum | solution.py:74
Sparse Core Ops, SparseCore 0:
  13.3 149.5 all-reduce.14
  165.4 33.0 reduce-scatter.6
  204.0 242.8 all-reduce.6
  473.3 133.1 all-reduce.8
  608.8 33.6 reduce-scatter.8
  644.6 63.9 all-reduce.10
  714.1 242.7 all-reduce.12
